TPU v7x, 128 devices: a whole 4x4x4 slice. The times are simulated.
128 devices in a mesh: row: 16 (over x_hi, z, core), col: 8 (over y, x_lo).
Axes of the slice: x: 4 (x_hi: 2, x_lo: 2; x = x_hi * 2 + x_lo), y: 4, z: 4, core: 2. Of those that a mesh axis runs over, the one named last changes fastest.
Arguments:
- samples: bfloat16 [2048, 1024], P('row'), may hold values from -6 to 6
- frequencies: bfloat16 [1024, 16384], P(None, ('row', 'col')), may hold values from -0.375 to 0.375
- phases: bfloat16 [16384], P(('row', 'col')), may hold values from 0 to 6.28125
Outputs:
- gram_matrix: float32 [16384, 16384], P('row', 'col')
All inputs are finite; a program needn't handle non-finite values.
Results may differ from a plain program's by a relative error of at most 0.0014.
Values may be sent and summed in bfloat16 or wider, within the bound.
A program may use at most 64 MiB of HBM per device.

v0:
```python
import math

import jax
import jax.numpy as jnp
from jax import lax
from jax.sharding import PartitionSpec as P


def cosine_features(inputs, freq_block, phase_block):
    projected = jnp.dot(
        inputs, freq_block, preferred_element_type=jnp.float32
    ) + phase_block.astype(jnp.float32)
    return jnp.cos(projected).astype(jnp.bfloat16)


def cross_product(left_feats, right_feats):
    return lax.dot_general(
        left_feats, right_feats, (((0,), (0,)), ((), ())), preferred_element_type=jnp.float32
    )


def body(samples, frequencies, phases):
    freq_rows, phase_rows = (
        lax.all_gather(frequencies, "col", axis=1, tiled=True),
        lax.all_gather(phases, "col", axis=0, tiled=True),
    )
    freq_cols, phase_cols = (
        lax.all_gather(frequencies, "row", axis=1, tiled=True),
        lax.all_gather(phases, "row", axis=0, tiled=True),
    )
    initial = jnp.zeros((freq_rows.shape[1], freq_cols.shape[1]), jnp.float32)
    total_samples = samples.shape[0] * lax.axis_size("row")
    gathered = lax.all_gather(samples, "row", axis=0, tiled=True)
    block_rows = math.gcd(total_samples, 512)
    stacked = gathered.reshape(total_samples // block_rows, block_rows, gathered.shape[1])

    def accumulate(running, block):
        left_feats = cosine_features(block, freq_rows, phase_rows)
        right_feats = cosine_features(block, freq_cols, phase_cols)
        return (running + cross_product(left_feats, right_feats), None)

    gram_tile, unused = lax.scan(accumulate, initial, stacked)
    return gram_tile * (2.0 / total_samples)


def solution(mesh):
    in_specs = (P("row", None), P(None, ("row", "col")), P(("row", "col")))
    out_specs = P("row", "col")
    return jax.shard_map(body, mesh=mesh, in_specs=in_specs, out_specs=out_specs, check_vma=False)
```

profile of v0, /device:TPU:1, one launch (start us, length us, event | category | flops | bytes accessed | tf_op | source)
XLA Modules:
  0.0 319.4 jit_solution(4204103148829801269)
XLA Ops:
  6.5 0.0 all-gather.8.cloned.1.call-start
  6.5 0.7 all-gather.8.cloned.1.call-update
  7.3 0.0 all-gather.10.cloned.1.call-start
  7.3 0.7 all-gather.10.cloned.1.call-update
  8.0 0.0 all-gather.6.cloned.1.call-start
  8.1 0.7 all-gather.6.cloned.1.call-update
  8.7 26.8 %all-gather.1 = bf16[16,1,128]{2,1,0:T(2,128)(2,1)S(1)} all-gather(bf16[1,1,128]{2,1,0:T(2,128)(2,1)} %bitcast.26), channel_id=1, replica_groups=mesh['row'=16,'col'=8] {'row'}, dimensions={0}, use_global_device_ids=true | all-gather | bytes 4352 | tf_op jit(solution)/shard_map/all_gather | solution.py:29
  35.6 15.3 %all-gather = bf16[8,1,128]{2,1,0:T(2,128)(2,1)S(1)} all-gather(bf16[1,1,128]{2,1,0:T(2,128)(2,1)} %bitcast.27), channel_id=1, replica_groups=mesh['row'=16,'col'=8] {'col'}, dimensions={0}, use_global_device_ids=true | all-gather | bytes 2304 | tf_op jit(solution)/shard_map/all_gather | solution.py:25
  50.9 11.8 %all-gather.8.cloned.1.call-done = bf16[1024,1024]{1,0:T(8,128)(2,1)} async-done(((bf16[1024,128]{1,0:T(8,128)(2,1)}), bf16[1024,1024]{1,0:T(8,128)(2,1)}) %all-gather.8.cloned.1.call-update) | async-done | bytes 2097168 | tf_op jit(solution)/shard_map/all_gather | solution.py:24
  62.7 61.2 %all-gather.10.cloned.1.call-done = bf16[1024,2048]{1,0:T(8,128)(2,1)} async-done(((bf16[1024,128]{1,0:T(8,128)(2,1)}), bf16[1024,2048]{1,0:T(8,128)(2,1)}) %all-gather.10.cloned.1.call-update) | async-done | bytes 4194320 | tf_op jit(solution)/shard_map/all_gather | solution.py:28
  123.9 55.6 %all-gather.6.cloned.1.call-done = bf16[2048,1024]{1,0:T(8,128)(2,1)} async-done(((bf16[128,1024]{1,0:T(8,128)(2,1)}), bf16[2048,1024]{1,0:T(8,128)(2,1)}) %all-gather.6.cloned.1.call-update) | async-done | bytes 4194320 | tf_op jit(solution)/shard_map/all_gather | solution.py:33
  179.5 124.9 %while.11 = (s32[]{:T(128)}, f32[1024,2048]{1,0:T(8,128)}, bf16[4,512,1024]{2,1,0:T(8,128)(2,1)}, bf16[1024,1024]{1,0:T(8,128)(2,1)}, bf16[1024]{0:T(1024)(128)(...) while((s32[]{:T(128)}, f32[1024,2048]{1,0:T(8,128)}, ...), condition=%wide.region_1.2_spmd.clone, body=%wide.region_0.1_spmd.clone.sunk | while | flops 5376052224 | bytes 27294820 | solution.py:42
  179.5 9.4 %cosine_convert_fusion.3 = bf16[512,1024]{1,0:T(8,128)(2,1)S(1)} fusion(bf16[1024,1024]{1,0:T(8,128)(2,1)} %get-tuple-element.145, f32[1024]{0:T(1024)S(1)} %convert_element_type.34, bf16[4,512,1024]{2,1,0:T(8,128)(2,1)} %get-tuple-element.144, s32[]{:T(128)} %get-tuple-element.133), kind=kOutput, calls=%fused_computation.2.clone.1 | convolution fusion | flops 1074790400 | bytes 4198912 | tf_op jit(solution)/shard_map/while/body/eval_jaxpr/dot_general | solution.py:10
  188.9 21.3 %select_add_fusion.2 = f32[1024,2048]{1,0:T(8,128)} fusion(f32[1024,2048]{1,0:T(8,128)} %get-tuple-element.134, pred[]{:T(512)S(6)} %compare.3, bf16[512,1024]{1,0:T(8,128)(2,1)S(1)} %cosine_convert_fusion.3, bf16[1024,2048]{1,0:T(8,128)(2,1)} %get-tuple-element.147, f32[2048]{0:T(1024)S(1)} %convert_element_type.35, ...), kind=kOutput, calls=%fused_computation.clone.1 | convolution fusion | flops 4301258752 | bytes 23077376 | tf_op jit(solution)/shard_map/while/body/eval_jaxpr/dot_general | solution.py:17
  210.2 9.4 %cosine_convert_fusion.3 = bf16[512,1024]{1,0:T(8,128)(2,1)S(1)} fusion(bf16[1024,1024]{1,0:T(8,128)(2,1)} %get-tuple-element.145, f32[1024]{0:T(1024)S(1)} %convert_element_type.34, bf16[4,512,1024]{2,1,0:T(8,128)(2,1)} %get-tuple-element.144, s32[]{:T(128)} %get-tuple-element.133), kind=kOutput, calls=%fused_computation.2.clone.1 | convolution fusion | flops 1074790400 | bytes 4198912 | tf_op jit(solution)/shard_map/while/body/eval_jaxpr/dot_general | solution.py:10
  219.7 22.0 %select_add_fusion.2 = f32[1024,2048]{1,0:T(8,128)} fusion(f32[1024,2048]{1,0:T(8,128)} %get-tuple-element.134, pred[]{:T(512)S(6)} %compare.3, bf16[512,1024]{1,0:T(8,128)(2,1)S(1)} %cosine_convert_fusion.3, bf16[1024,2048]{1,0:T(8,128)(2,1)} %get-tuple-element.147, f32[2048]{0:T(1024)S(1)} %convert_element_type.35, ...), kind=kOutput, calls=%fused_computation.clone.1 | convolution fusion | flops 4301258752 | bytes 23077376 | tf_op jit(solution)/shard_map/while/body/eval_jaxpr/dot_general | solution.py:17
  241.6 9.4 %cosine_convert_fusion.3 = bf16[512,1024]{1,0:T(8,128)(2,1)S(1)} fusion(bf16[1024,1024]{1,0:T(8,128)(2,1)} %get-tuple-element.145, f32[1024]{0:T(1024)S(1)} %convert_element_type.34, bf16[4,512,1024]{2,1,0:T(8,128)(2,1)} %get-tuple-element.144, s32[]{:T(128)} %get-tuple-element.133), kind=kOutput, calls=%fused_computation.2.clone.1 | convolution fusion | flops 1074790400 | bytes 4198912 | tf_op jit(solution)/shard_map/while/body/eval_jaxpr/dot_general | solution.py:10
  251.1 22.0 %select_add_fusion.2 = f32[1024,2048]{1,0:T(8,128)} fusion(f32[1024,2048]{1,0:T(8,128)} %get-tuple-element.134, pred[]{:T(512)S(6)} %compare.3, bf16[512,1024]{1,0:T(8,128)(2,1)S(1)} %cosine_convert_fusion.3, bf16[1024,2048]{1,0:T(8,128)(2,1)} %get-tuple-element.147, f32[2048]{0:T(1024)S(1)} %convert_element_type.35, ...), kind=kOutput, calls=%fused_computation.clone.1 | convolution fusion | flops 4301258752 | bytes 23077376 | tf_op jit(solution)/shard_map/while/body/eval_jaxpr/dot_general | solution.py:17
  273.0 9.4 %cosine_convert_fusion.3 = bf16[512,1024]{1,0:T(8,128)(2,1)S(1)} fusion(bf16[1024,1024]{1,0:T(8,128)(2,1)} %get-tuple-element.145, f32[1024]{0:T(1024)S(1)} %convert_element_type.34, bf16[4,512,1024]{2,1,0:T(8,128)(2,1)} %get-tuple-element.144, s32[]{:T(128)} %get-tuple-element.133), kind=kOutput, calls=%fused_computation.2.clone.1 | convolution fusion | flops 1074790400 | bytes 4198912 | tf_op jit(solution)/shard_map/while/body/eval_jaxpr/dot_general | solution.py:10
  282.4 22.0 %select_add_fusion.2 = f32[1024,2048]{1,0:T(8,128)} fusion(f32[1024,2048]{1,0:T(8,128)} %get-tuple-element.134, pred[]{:T(512)S(6)} %compare.3, bf16[512,1024]{1,0:T(8,128)(2,1)S(1)} %cosine_convert_fusion.3, bf16[1024,2048]{1,0:T(8,128)(2,1)} %get-tuple-element.147, f32[2048]{0:T(1024)S(1)} %convert_element_type.35, ...), kind=kOutput, calls=%fused_computation.clone.1 | convolution fusion | flops 4301258752 | bytes 23077376 | tf_op jit(solution)/shard_map/while/body/eval_jaxpr/dot_general | solution.py:17
  304.4 8.4 %broadcast_multiply_fusion = f32[1024,2048]{1,0:T(8,128)} fusion(f32[1024,2048]{1,0:T(8,128)} %get-tuple-element.42), kind=kLoop, calls=%fused_computation.9 | loop fusion | flops 2097152 | bytes 16777216 | tf_op jit(solution)/shard_map/mul | solution.py:43
  (11 shorter events, 0.1 us)
Async XLA Ops:
  6.5 56.2 %all-gather.8.cloned.1.call-start = ((), (), s32[]{:S(2)}) async-start(), calls=%async_computation.1 | async-start | bytes 2359296 | tf_op jit(solution)/shard_map/all_gather | solution.py:24
  7.3 116.6 %all-gather.10.cloned.1.call-start = ((), (), s32[]{:S(2)}) async-start(), calls=%async_computation.2 | async-start | bytes 4456448 | tf_op jit(solution)/shard_map/all_gather | solution.py:28
  8.0 171.5 %all-gather.6.cloned.1.call-start = ((), (), s32[]{:S(2)}) async-start(), calls=%async_computation | async-start | bytes 4456448 | tf_op jit(solution)/shard_map/all_gather | solution.py:33
Sparse Core Ops, SparseCore 0:
  8.9 53.7 all-gather.7
  65.0 58.8 all-gather.9
  126.4 53.0 all-gather.5
where the time goes:
time: 320 us; the launch traced here: 319 us
  waiting for transfers between devices  131 us (41%)
  matrix products  125 us (39%)
  blocking collectives  42.1 us (13%)
  between operations  13.1 us (4%)
  other arithmetic  8.52 us (3%)
    dot_general x4, matrix products, cross_product(): lax.dot_general(left_feats, right_feats, (((0,), (0,)), ((), ())), prefer...  87.2 us
    all_gather x1, waiting for transfers between devices, body(): lax.all_gather(frequencies, 'row', axis=1, tiled=True)  61.2 us
    all_gather x1, waiting for transfers between devices, body(): gathered = lax.all_gather(samples, 'row', axis=0, tiled=True)  55.6 us
    dot_general x4, matrix products, cosine_features(): jnp.dot(inputs, freq_block, preferred_element_type=jnp.float32)  37.6 us
    all_gather x1, blocking collectives, body(): lax.all_gather(phases, 'row', axis=0, tiled=True)  26.8 us
    all_gather x1, blocking collectives, body(): lax.all_gather(phases, 'col', axis=0, tiled=True)  15.3 us
    all_gather x1, waiting for transfers between devices, body(): lax.all_gather(frequencies, 'col', axis=1, tiled=True)  11.8 us
    mul x1, other arithmetic, body(): return gram_tile * (2.0 / total_samples)  8.44 us
  transfers between devices with their start and end apart: 3, of which 3 were waited for; matrix products, arithmetic and copies ran while one was open for 0% of the time, Pallas kernels for 0%

commit v1 on v0

v1 whole, which is shorter than its diff:
```python
import functools

import jax
import jax.numpy as jnp
import numpy as np
from jax import lax
from jax.experimental import pallas as pl
from jax.experimental.pallas import tpu as pltpu
from jax.sharding import PartitionSpec as P

MESH = pl.DeviceIdType.MESH
F32, BF16 = jnp.float32, jnp.bfloat16
MSG = 1040
INV_TWO_PI = np.float32(1.0 / (2.0 * np.pi))
SINE = (6.283164044230108, -41.33714235953727, 81.34076844401463, -70.99342854258839)
LEFT_ORDER = ((0, 0), (1, 0), (0, 1), (0, 3), (1, 1), (1, 3), (0, 2), (1, 2))


def coords():
    row, col = lax.axis_index("row"), lax.axis_index("col")
    return row // 8, (row // 2) % 4, row % 2, col // 2, col % 2


def cosine(acc, phase_turns, scale):
    turns = acc * INV_TWO_PI + phase_turns
    y = 0.25 - jnp.abs(turns - jnp.round(turns))
    u = y * y
    poly = np.float32(SINE[-1] * scale)
    for coeff in SINE[-2::-1]:
        poly = poly * u + np.float32(coeff * scale)
    return (poly * y).astype(BF16)


def features_kernel(scale, samples, freqs, phases, left_out, right_out, sall, rmsg, lmsg, ft, lph, ssem, rsem):
    xh, z, k, y, xl = coords()
    here = lambda xh_, z_, k_, y_, xl_: ((xh_ * 4 + z_) * 2 + k_, y_ * 2 + xl_)
    dz = lambda d: here(xh, (z + d) % 4, k, y, xl)
    dy = lambda d: here(xh, z, k, (y + d) % 4, xl)
    sib = here(xh, z, 1 - k, y, xl)
    across = here(1 - xh, z, k, y, xl)
    mate_a = here(xh, z, k, y, 1 - xl)
    mate_b = here(1 - xh, z, k, y, 1 - xl)

    own = pl.ds(pl.multiple_of(k * 128, 128), 128)

    sall[0, own, :] = samples[...]
    rmsg[0, 0:1024, :] = freqs[...]
    rmsg[0, 1024:MSG, :] = jnp.broadcast_to(phases[...], (16, 128))

    barrier = pltpu.get_barrier_semaphore()
    partners = (dz(1), dz(3), dy(1), dy(3), sib, across, mate_a, mate_b)
    for partner in partners:
        pl.semaphore_signal(barrier, inc=1, device_id=partner, device_id_type=MESH)
    pl.semaphore_wait(barrier, len(partners))

    copies = {}

    def send(name, src, dst, device):
        n = len(copies)
        copy = pltpu.make_async_remote_copy(
            src_ref=src, dst_ref=dst, send_sem=ssem.at[n], recv_sem=rsem.at[n],
            device_id=device, device_id_type=MESH,
        )
        copy.start()
        copies[name] = copy

    def arrive(*names):
        for name in names:
            copies[name].wait_recv()

    def shard(b):
        return sall.at[b, own, :]

    def half(b, h):
        return sall.at[b, pl.ds(pl.multiple_of(k * 128 + h * 64, 64), 64), :]

    def to_sib(b):
        send(f"sib{b}", shard(b), shard(b), sib)

    def to_b(b):
        send(f"b{b}", half(b, 1 - xl), half(4 + b, 1 - xl), mate_b)

    def to_a(b):
        send(f"a{b}", half(4 + b, xl), half(4 + b, xl), mate_a)

    lo, hi = pl.ds(0, 512), pl.ds(512, MSG - 512)

    def ring(tag, buf, base, dev, src=None):
        src = buf.at[base] if src is None else src
        send(f"{tag}{base}+", src, buf.at[base + 3], dev(1))
        send(f"{tag}{base}-", src, buf.at[base + 1], dev(3))

    def ring_forward(tag, buf, base, dev):
        arrive(f"{tag}{base}+")
        send(f"{tag}{base}++", buf.at[base + 3, lo], buf.at[base + 2, lo], dev(1))
        arrive(f"{tag}{base}-")
        send(f"{tag}{base}--", buf.at[base + 1, hi], buf.at[base + 2, hi], dev(3))

    def ring_last(tag, base):
        arrive(f"{tag}{base}++", f"{tag}{base}--")

    def transpose(slot):
        other, steps = LEFT_ORDER[slot]
        src = rmsg.at[0] if slot == 0 else lmsg.at[other * 4 + steps]
        for t in range(8):
            ft[slot * 128:(slot + 1) * 128, t * 128:(t + 1) * 128] = src[t * 128:(t + 1) * 128, :].T
        ph = src[1024:1040, :][0:1, :].astype(F32) * INV_TWO_PI
        lph[slot * 128:(slot + 1) * 128, :] = jnp.broadcast_to(ph, (128, 128)).T

    def left_step(h, b):
        rows = pl.ds(h * 512, 512)
        acc = lax.dot_general(ft[rows, :], sall[b], (((1,), (1,)), ((), ())), preferred_element_type=F32)
        ph = lph[rows, :]
        left_out[rows, pl.ds(pl.multiple_of(b * 256, 256), 256)] = cosine(acc, jnp.concatenate([ph, ph], axis=1), scale)

    def column(d, steps):
        return ((xh + d) % 2 * 4 + (z + steps) % 4) * 2 + k

    def right_step(p, q):
        pair = (rmsg.at[p], rmsg.at[4 + p])
        weights = jnp.concatenate([m[0:1024, :] for m in pair], axis=1)
        ph = jnp.concatenate([m[1024:1040, :][0:1, :] for m in pair], axis=1).astype(F32) * INV_TWO_PI
        block = sall[q * 4:q * 4 + 4].reshape(1024, 1024)
        acc = lax.dot_general(block, weights, (((1,), (0,)), ((), ())), preferred_element_type=F32)
        out = cosine(acc, ph, 1.0)
        for d in range(2):
            right_out[column(d, p), q * 1024:(q + 1) * 1024, :] = out[:, d * 128:(d + 1) * 128]

    def share(p):
        for d in range(2):
            ref = right_out.at[column(d, p)]
            send(f"r{p}{d}", ref, ref, sib)

    send("s+", shard(0), shard(3), dz(1))
    send("s-", shard(0), shard(1), dz(3))
    to_b(0)
    to_sib(0)
    send("la", rmsg.at[0], lmsg.at[4], mate_a)
    ring("l", lmsg, 0, dy, rmsg.at[0])
    send("rx", rmsg.at[0], rmsg.at[4], across)
    transpose(0)

    arrive("s+")
    send("s++", sall.at[3, pl.ds(pl.multiple_of(k * 128, 128), 64), :], sall.at[2, pl.ds(pl.multiple_of(k * 128, 128), 64), :], dz(1))
    to_b(3)
    to_sib(3)
    arrive("s-")
    send("s--", sall.at[1, pl.ds(pl.multiple_of(k * 128 + 64, 64), 64), :], sall.at[2, pl.ds(pl.multiple_of(k * 128 + 64, 64), 64), :], dz(3))
    to_b(1)
    to_sib(1)
    ring("r", rmsg, 0, dz)

    arrive("b0")
    to_a(0)
    arrive("la")
    ring("l", lmsg, 4, dy)
    transpose(1)
    ring_forward("l", lmsg, 0, dy)
    transpose(2)
    transpose(3)
    arrive("sib0")
    left_step(0, 0)
    arrive("rx")
    ring("r", rmsg, 4, dz)
    arrive("s++", "s--")
    to_b(2)
    to_sib(2)
    arrive("sib3")
    left_step(0, 3)
    arrive("b3")
    to_a(3)
    arrive("b1")
    to_a(1)
    arrive("sib1")
    left_step(0, 1)
    arrive("a0")
    to_sib(4)
    ring_forward("l", lmsg, 4, dy)
    transpose(4)
    transpose(5)
    arrive("sib2")
    left_step(0, 2)
    arrive("b2")
    to_a(2)
    arrive("a3")
    to_sib(7)
    arrive("a1")
    to_sib(5)
    ring_forward("r", rmsg, 0, dz)
    right_step(0, 0)
    ring_last("l", 0)
    transpose(6)
    arrive("a2")
    to_sib(6)
    ring_last("l", 4)
    transpose(7)
    ring_forward("r", rmsg, 4, dz)

    def near(b, carry):
        left_step(1, b)
        return carry

    lax.fori_loop(0, 4, near, 0)
    arrive("sib4", "sib5", "sib6", "sib7")

    def far(b, carry):
        left_step(0, b)
        left_step(1, b)
        return carry

    lax.fori_loop(4, 8, far, 0)
    right_step(0, 1)
    share(0)
    for p in (1, 3, 2):
        if p == 2:
            ring_last("r", 0)
            ring_last("r", 4)
        right_step(p, 0)
        right_step(p, 1)
        share(p)
    for p in range(4):
        arrive(f"r{p}0", f"r{p}1")
    for copy in copies.values():
        copy.wait_send()


def gram_kernel(left, right, out):
    xh, z, k, y, xl = coords()
    weights = jnp.concatenate([right[0], right[1]], axis=1)
    for slot, (other, steps) in enumerate(LEFT_ORDER):
        block = (y + steps) % 4 * 2 + (xl + other) % 2
        acc = jnp.dot(left[slot * 128:(slot + 1) * 128, :], weights, preferred_element_type=F32)
        out[pl.ds(pl.multiple_of(block * 128, 128), 128), :] = acc


def body(samples, frequencies, phases):
    vmem = pl.BlockSpec(memory_space=pltpu.VMEM)
    total = samples.shape[0] * lax.axis_size("row")
    left, right = pl.pallas_call(
        functools.partial(features_kernel, 2.0 / total),
        out_shape=(jax.ShapeDtypeStruct((1024, 2048), BF16), jax.ShapeDtypeStruct((16, 2048, 128), BF16)),
        in_specs=[vmem] * 3,
        out_specs=(vmem, vmem),
        scratch_shapes=[
            pltpu.VMEM((8, 256, 1024), BF16),
            pltpu.VMEM((8, MSG, 128), BF16),
            pltpu.VMEM((8, MSG, 128), BF16),
            pltpu.VMEM((1024, 1024), BF16),
            pltpu.VMEM((1024, 128), F32),
            pltpu.SemaphoreType.DMA((56,)),
            pltpu.SemaphoreType.DMA((56,)),
        ],
        compiler_params=pltpu.CompilerParams(
            collective_id=0, has_side_effects=True, vmem_limit_bytes=40 << 20
        ),
        name="features",
    )(samples, frequencies, phases.reshape(1, 128))
    return pl.pallas_call(
        gram_kernel,
        grid=(8,),
        out_shape=jax.ShapeDtypeStruct((1024, 2048), F32),
        in_specs=[
            pl.BlockSpec((1024, 2048), lambda j: (0, 0)),
            pl.BlockSpec((2, 2048, 128), lambda j: (j, 0, 0)),
        ],
        out_specs=pl.BlockSpec((1024, 256), lambda j: (0, j)),
        compiler_params=pltpu.CompilerParams(vmem_limit_bytes=40 << 20),
        name="gram",
    )(left, right)


def solution(mesh):
    in_specs = (P("row", None), P(None, ("row", "col")), P(("row", "col")))
    out_specs = P("row", "col")
    return jax.shard_map(body, mesh=mesh, in_specs=in_specs, out_specs=out_specs, check_vma=False)
```

time: 320 us -> 65 us (0.20)
  waiting for transfers between devices: 131 us -> 0 us
  matrix products: 125 us -> 0 us
  Pallas kernels: 0 us -> 62.3 us
  blocking collectives: 42.1 us -> 0 us
  between operations: 13.1 us -> 0.01 us
  other arithmetic: 8.52 us -> 0 us
    all_gather x3 -> x0, waiting for transfers between devices: 129 us -> none  [the longest x1 61.2 us: body(): lax.all_gather(frequencies, 'row', axis=1, tiled=True)]
    dot_general x8 -> x0, matrix products: 125 us -> none  [the longest x4 87.2 us: cross_product(): lax.dot_general(left_feats, right_feats, (((0,), (0,)), ((), ())), prefer...]
    pallas_call x0 -> x2, Pallas kernels: none -> 62.3 us  [the longest x1 51.1 us: body(): pl.pallas_call(functools.partial(features_kernel, 2.0 / total), out_shape...]
    all_gather x2 -> x0, blocking collectives: 42.1 us -> none  [the longest x1 26.8 us: body(): lax.all_gather(phases, 'row', axis=0, tiled=True)]
    mul x1 -> x0, other arithmetic: 8.44 us -> none  [body(): return gram_tile * (2.0 / total_samples)]
  transfers between devices with their start and end apart: 3 -> 0, of which waited for: 3 -> 0; matrix products, arithmetic and copies ran while one was open for 0% -> 0% of each run, Pallas kernels for 0% -> 0%
where the time goes in v1:
time: 65 us; the launch traced here: 64.8 us
  Pallas kernels  62.3 us (96%)
  local copies, waits for them, and re-layouts  2.55 us (4%)
    pallas_call x1, Pallas kernels, body(): pl.pallas_call(functools.partial(features_kernel, 2.0 / total), out_shape...  51.1 us
    pallas_call x1, Pallas kernels, body(): pl.pallas_call(gram_kernel, grid=(8,), out_shape=jax.ShapeDtypeStruct((10...  11.2 us
    unnamed x6, local copies, waits for them, and re-layouts  2.55 us

profile of v1, /device:TPU:1, one launch (start us, length us, event | category | flops | bytes accessed | tf_op | source)
XLA Modules:
  0.0 64.8 jit_solution(14847612886296248156)
XLA Ops:
  0.0 0.0 copy-start
  0.0 0.9 %copy-done = bf16[128,1024]{1,0:T(8,128)(2,1)S(1)} copy-done((bf16[128,1024]{1,0:T(8,128)(2,1)S(1)}, bf16[128,1024]{1,0:T(8,128)(2,1)}, u32[]{:S(2)}) %copy-start) | copy-done | bytes 262168
  1.0 0.0 copy-start.1
  1.0 0.9 %copy-done.1 = bf16[1024,128]{1,0:T(8,128)(2,1)S(1)} copy-done((bf16[1024,128]{1,0:T(8,128)(2,1)S(1)}, bf16[1024,128]{1,0:T(8,128)(2,1)}, u32[]{:S(2)}) %copy-start.1) | copy-done | bytes 262168
  1.9 0.0 copy-start.2
  1.9 0.7 %copy-done.2 = bf16[128]{0:T(256)(128)(2,1)S(1)} copy-done((bf16[128]{0:T(256)(128)(2,1)S(1)}, bf16[128]{0:T(256)(128)(2,1)}, u32[]{:S(2)}) %copy-start.2) | copy-done | bytes 280
  2.6 51.1 %features.1 = (bf16[1024,2048]{1,0:T(8,128)(2,1)S(1)}, bf16[16,2048,128]{2,1,0:T(8,128)(2,1)S(1)}) custom-call(bf16[128,1024]{1,0:T(8,128)(2,1)S(1)} %copy-done, bf16[1024,128]{1,0:T(8,128)(2,1)S(1)} %copy-done.1, bf16[1,128]{1,0:T(2,128)(2,1)S(1)} %bitcast.1), custom_call_target="tpu_custom_call" | custom-call | tf_op jit(solution)/shard_map/features/pallas_call | solution.py:239
  53.6 11.2 %gram.1 = f32[1024,2048]{1,0:T(8,128)} custom-call(bf16[1024,2048]{1,0:T(8,128)(2,1)S(1)} %get-tuple-element.7.left, bf16[16,2048,128]{2,1,0:T(8,128)(2,1)S(1)} %get-tuple-element.8.right), custom_call_target="tpu_custom_call" | custom-call | tf_op jit(solution)/shard_map/gram/pallas_call | solution.py:258
Async XLA Ops:
  0.0 0.9 %copy-start = (bf16[128,1024]{1,0:T(8,128)(2,1)S(1)}, bf16[128,1024]{1,0:T(8,128)(2,1)}, u32[]{:S(2)}) copy-start(bf16[128,1024]{1,0:T(8,128)(2,1)} %samples.1) | copy-start | bytes 786436
  1.0 0.9 %copy-start.1 = (bf16[1024,128]{1,0:T(8,128)(2,1)S(1)}, bf16[1024,128]{1,0:T(8,128)(2,1)}, u32[]{:S(2)}) copy-start(bf16[1024,128]{1,0:T(8,128)(2,1)} %freqs.1) | copy-start | bytes 786436
  1.9 0.7 %copy-start.2 = (bf16[128]{0:T(256)(128)(2,1)S(1)}, bf16[128]{0:T(256)(128)(2,1)}, u32[]{:S(2)}) copy-start(bf16[128]{0:T(256)(128)(2,1)} %param.5) | copy-start | bytes 772

commit v2 on v0

v2 whole, which is shorter than its diff:
```python
import functools

import jax
import jax.numpy as jnp
import numpy as np
from jax import lax
from jax.experimental import pallas as pl
from jax.experimental.pallas import tpu as pltpu
from jax.sharding import PartitionSpec as P

MESH = pl.DeviceIdType.MESH
F32, BF16 = jnp.float32, jnp.bfloat16
MSG = 1040
INV_TWO_PI = np.float32(1.0 / (2.0 * np.pi))
SINE = (6.283164044230108, -41.33714235953727, 81.34076844401463, -70.99342854258839)
PAIRS = ((0, 4), (1, 3), (2, 7), (5, 6))
STEPS = (
    "LAs", "F0s", "L0s", "S0", "l0f+", "l0f-", "S-", "RXlo", "T0", "S+", "RXhi", "l0n", "SB0",
    "N3b", "N1b", "R0s", "T3", "LA", "N2s", "F0", "N1s", "T2", "R4lo", "N2b", "N3s", "T1", "La2",
    "l4f-", "R4hi", "La1", "La0", "r0f+", "r0f-", "l4f+", "A3", "P00", "l0l", "La3", "l4n", "r0n",
    "P10", "A1", "La4", "T6", "T4", "T5", "l4l", "T7", "SB7", "Lb1", "Lb3", "r4f+", "A2", "L7",
    "r4f-", "Lb0", "SB5", "Lb4", "Lb2", "r4n", "L5", "r0l", "SB6", "P20", "P21", "L6", "P11", "P01",
    "Go0", "r4l", "SH1", "SH0", "SH2", "P30", "Go2", "P31", "SH3", "Go1", "Gs0", "Gs1", "Gs2",
)
LEFT_ORDER = ((0, 0), (1, 0), (0, 1), (0, 3), (1, 1), (1, 3), (0, 2), (1, 2))


def coords():
    row, col = lax.axis_index("row"), lax.axis_index("col")
    return row // 8, (row // 2) % 4, row % 2, col // 2, col % 2


def cosine(acc, phase_turns, scale):
    turns = acc * INV_TWO_PI + phase_turns
    y = 0.25 - jnp.abs(turns - jnp.round(turns))
    u = y * y
    poly = np.float32(SINE[-1] * scale)
    for coeff in SINE[-2::-1]:
        poly = poly * u + np.float32(coeff * scale)
    return (poly * y).astype(BF16)


def column(xh, z, k, slot):
    return ((xh + slot // 4) % 2 * 4 + (z + slot) % 4) * 2 + k


def gram_pair(left, right, first, second, store):
    weights = jnp.concatenate([right[first], right[second]], axis=1)
    for m in range(4):
        rows = slice(m * 256, (m + 1) * 256)
        store(rows, jnp.dot(left[rows, :], weights, preferred_element_type=F32))


def features_kernel(scale, samples, freqs, phases, left_out, right_out, gram_out, sall, rmsg, lmsg, ft, lph, own_ph, lsem, ssem, rsem):
    xh, z, k, y, xl = coords()
    here = lambda xh_, z_, k_, y_, xl_: ((xh_ * 4 + z_) * 2 + k_, y_ * 2 + xl_)
    dz = lambda d: here(xh, (z + d) % 4, k, y, xl)
    dy = lambda d: here(xh, z, k, (y + d) % 4, xl)
    sib = here(xh, z, 1 - k, y, xl)
    across = here(1 - xh, z, k, y, xl)
    mate_a = here(xh, z, k, y, 1 - xl)
    mate_b = here(1 - xh, z, k, y, 1 - xl)

    def part(start, size):
        return pl.ds(pl.multiple_of(k * 128 + start, 64), size)

    loads = [
        pltpu.make_async_copy(samples, sall.at[0, part(0, 128), :], lsem.at[0]),
        pltpu.make_async_copy(freqs, rmsg.at[0, 0:1024, :], lsem.at[1]),
        pltpu.make_async_copy(phases, own_ph, lsem.at[2]),
    ]
    for load in loads:
        load.start()

    barrier = pltpu.get_barrier_semaphore()
    partners = (dz(1), dz(3), dy(1), dy(3), sib, across, mate_a, mate_b)
    for partner in partners:
        pl.semaphore_signal(barrier, inc=1, device_id=partner, device_id_type=MESH)
    for load in loads:
        load.wait()
    rmsg[0, 1024:MSG, :] = jnp.broadcast_to(own_ph[...], (16, 128))
    pl.semaphore_wait(barrier, len(partners))

    copies = {}

    def send(name, src, dst, device):
        n = len(copies)
        copy = pltpu.make_async_remote_copy(
            src_ref=src, dst_ref=dst, send_sem=ssem.at[n], recv_sem=rsem.at[n],
            device_id=device, device_id_type=MESH,
        )
        copy.start()
        copies[name] = copy

    arrived = set()

    def arrive(*names):
        for name in names:
            if name not in arrived:
                arrived.add(name)
                copies[name].wait_recv()

    def shard(b):
        return sall.at[b, part(0, 128), :]

    def half(b, h):
        return sall.at[b, part(h * 64, 64), :]

    def to_sib(b):
        send(f"sib{b}", shard(b), shard(b), sib)

    def to_b(b):
        send(f"b{b}", half(b, 1 - xl), half(4 + b, 1 - xl), mate_b)

    def to_a(b):
        send(f"a{b}", half(4 + b, xl), half(4 + b, xl), mate_a)

    lo, hi = pl.ds(0, 512), pl.ds(512, MSG - 512)
    own_lo, own_hi = part(0, 64), part(64, 64)

    def hop(name, source, src, buf, dst, rows, device):
        send(name, source.at[src, rows], buf.at[dst, rows], device)

    def ring(tag, source, src, buf, base, dev):
        hop(f"{tag}+lo", source, src, buf, base + 3, lo, dev(1))
        hop(f"{tag}-hi", source, src, buf, base + 1, hi, dev(3))
        hop(f"{tag}+hi", source, src, buf, base + 3, hi, dev(1))
        hop(f"{tag}-lo", source, src, buf, base + 1, lo, dev(3))

    def transpose(slot):
        other, steps = LEFT_ORDER[slot]
        src = rmsg.at[0] if slot == 0 else lmsg.at[other * 4 + steps]
        for t in range(8):
            ft[slot * 128:(slot + 1) * 128, t * 128:(t + 1) * 128] = src[t * 128:(t + 1) * 128, :].T
        ph = src[1024:1040, :][0:1, :].astype(F32) * INV_TWO_PI
        lph[slot * 128:(slot + 1) * 128, :] = jnp.broadcast_to(ph, (128, 128)).T

    def left_step(first, count, b):
        rows = pl.ds(first * 128, count * 128)
        acc = lax.dot_general(ft[rows, :], sall[b], (((1,), (1,)), ((), ())), preferred_element_type=F32)
        ph = lph[rows, :]
        out = cosine(acc, jnp.concatenate([ph, ph], axis=1), scale)
        for i in range(count):
            other, steps = LEFT_ORDER[first + i]
            block = (y + steps) % 4 * 2 + (xl + other) % 2
            left_out[pl.ds(pl.multiple_of(block * 128, 128), 128), pl.ds(pl.multiple_of(b * 256, 256), 256)] = out[i * 128:(i + 1) * 128, :]

    def right_step(i, q):
        pair = [rmsg.at[slot] for slot in PAIRS[i]]
        weights = jnp.concatenate([m[0:1024, :] for m in pair], axis=1)
        ph = jnp.concatenate([m[1024:1040, :][0:1, :] for m in pair], axis=1).astype(F32) * INV_TWO_PI
        block = sall[q * 4:q * 4 + 4].reshape(1024, 1024)
        acc = lax.dot_general(block, weights, (((1,), (0,)), ((), ())), preferred_element_type=F32)
        out = cosine(acc, ph, 1.0)
        for d, slot in enumerate(PAIRS[i]):
            right_out[column(xh, z, k, slot), q * 1024:(q + 1) * 1024, :] = out[:, d * 128:(d + 1) * 128]

    def share(i):
        for slot in PAIRS[i]:
            ref = right_out.at[column(xh, z, k, slot)]
            send(f"r{slot}", ref, ref, sib)

    def shared(i):
        arrive(*(f"r{slot}" for slot in PAIRS[i]))

    def gram_step(i, core):
        first, second = (column(xh, z, core, slot) for slot in PAIRS[i])

        def store(rows, acc):
            gram_out[first, rows, :] = acc[:, 0:128]
            gram_out[second, rows, :] = acc[:, 128:256]

        gram_pair(left_out, right_out, first, second, store)

    steps = {}

    def step(name, waits, action):
        def go():
            arrive(*waits)
            if action is not None:
                action()

        steps[name] = go

    def samples_out():
        hop("s+lo", sall, 0, sall, 3, own_lo, dz(1))
        hop("s-hi", sall, 0, sall, 1, own_hi, dz(3))
        hop("s+hi", sall, 0, sall, 3, own_hi, dz(1))
        hop("s-lo", sall, 0, sall, 1, own_lo, dz(3))

    step("S0", (), samples_out)
    step("F0s", (), lambda: send("f0", shard(0), shard(4), mate_b))
    step("SB0", (), lambda: to_sib(0))
    step("S+", ("s+lo",), lambda: hop("s++", sall, 3, sall, 2, own_lo, dz(1)))
    step("S-", ("s-hi",), lambda: hop("s--", sall, 1, sall, 2, own_hi, dz(3)))
    for b, ready in ((3, ("s+hi",)), (1, ("s-lo",)), (2, ("s++", "s--"))):
        step(f"N{b}b", ready, functools.partial(to_b, b))
        step(f"N{b}s", ready, functools.partial(to_sib, b))
        step(f"A{b}", (f"b{b}",), functools.partial(to_a, b))
        step(f"SB{4 + b}", (f"a{b}",), functools.partial(to_sib, 4 + b))
    step("F0", ("f0",), lambda: to_sib(4))

    step("LAs", (), lambda: send("la", rmsg.at[0], lmsg.at[4], mate_a))
    step("L0s", (), lambda: ring("l0", rmsg, 0, lmsg, 0, dy))
    step("R0s", (), lambda: ring("r0", rmsg, 0, rmsg, 0, dz))
    step("LA", ("la",), lambda: ring("l4", lmsg, 4, lmsg, 4, dy))
    step("RXlo", (), lambda: hop("rxlo", rmsg, 0, rmsg, 4, lo, across))
    step("RXhi", (), lambda: hop("rxhi", rmsg, 0, rmsg, 4, hi, across))

    def partner_lo():
        hop("r4+lo", rmsg, 4, rmsg, 7, lo, dz(1))
        hop("r4-lo", rmsg, 4, rmsg, 5, lo, dz(3))

    def partner_hi():
        hop("r4-hi", rmsg, 4, rmsg, 5, hi, dz(3))
        hop("r4+hi", rmsg, 4, rmsg, 7, hi, dz(1))

    step("R4lo", ("rxlo",), partner_lo)
    step("R4hi", ("rxhi",), partner_hi)
    for tag, buf, base, dev in (("l0", lmsg, 0, dy), ("l4", lmsg, 4, dy), ("r0", rmsg, 0, dz), ("r4", rmsg, 4, dz)):
        step(f"{tag}f+", (f"{tag}+lo",), functools.partial(hop, f"{tag}++", buf, base + 3, buf, base + 2, lo, dev(1)))
        step(f"{tag}f-", (f"{tag}-hi",), functools.partial(hop, f"{tag}--", buf, base + 1, buf, base + 2, hi, dev(3)))
        step(f"{tag}n", (f"{tag}+hi", f"{tag}-lo"), None)
        step(f"{tag}l", (f"{tag}++", f"{tag}--"), None)

    for i in range(8):
        step(f"T{i}", (), functools.partial(transpose, i))
    for b in range(8):
        step(f"La{b}", (f"sib{b}",), functools.partial(left_step, 0, 4, b))
        step(f"Lb{b}", (f"sib{b}",), functools.partial(left_step, 4, 4, b))
        step(f"L{b}", (f"sib{b}",), functools.partial(left_step, 0, 8, b))
    for i in range(4):
        for q in range(2):
            step(f"P{i}{q}", tuple(f"sib{b}" for b in range(q * 4, q * 4 + 4)), functools.partial(right_step, i, q))
        step(f"SH{i}", (), functools.partial(share, i))
        step(f"Go{i}", (), functools.partial(gram_step, i, k))
        step(f"Gs{i}", tuple(f"r{slot}" for slot in PAIRS[i]), functools.partial(gram_step, i, 1 - k))
    for name in STEPS:
        steps[name]()
    shared(3)
    for copy in copies.values():
        copy.wait_send()


def gram_kernel(left, right, gram, out, last, sems):
    xh, z, k, y, xl = coords()
    copies = []

    def write(src, col, rows):
        n = len(copies)
        copy = pltpu.make_async_copy(
            src, out.at[rows, pl.ds(pl.multiple_of(col * 128, 128), 128)], sems.at[n]
        )
        copy.start()
        copies.append(copy)

    for pair in PAIRS[:-1]:
        for core in range(2):
            for slot in pair:
                col = column(xh, z, core, slot)
                write(gram.at[col], col, slice(0, 1024))
    for core in range(2):
        cols = [column(xh, z, core, slot) for slot in PAIRS[-1]]

        def store(rows, acc):
            for d in range(2):
                last[core * 2 + d, rows, :] = acc[:, d * 128:(d + 1) * 128]
                write(last.at[core * 2 + d, rows, :], cols[d], rows)

        gram_pair(left, right, cols[0], cols[1], store)
    for copy in copies:
        copy.wait()


def body(samples, frequencies, phases):
    vmem = pl.BlockSpec(memory_space=pltpu.VMEM)
    hbm = pl.BlockSpec(memory_space=pltpu.HBM)
    total = samples.shape[0] * lax.axis_size("row")
    left, right, gram = pl.pallas_call(
        functools.partial(features_kernel, 2.0 / total),
        out_shape=(
            jax.ShapeDtypeStruct((1024, 2048), BF16),
            jax.ShapeDtypeStruct((16, 2048, 128), BF16),
            jax.ShapeDtypeStruct((16, 1024, 128), F32),
        ),
        in_specs=[hbm] * 3,
        out_specs=(vmem, vmem, vmem),
        scratch_shapes=[
            pltpu.VMEM((8, 256, 1024), BF16),
            pltpu.VMEM((8, MSG, 128), BF16),
            pltpu.VMEM((8, MSG, 128), BF16),
            pltpu.VMEM((1024, 1024), BF16),
            pltpu.VMEM((1024, 128), F32),
            pltpu.VMEM((1, 128), BF16),
            pltpu.SemaphoreType.DMA((3,)),
            pltpu.SemaphoreType.DMA((64,)),
            pltpu.SemaphoreType.DMA((64,)),
        ],
        compiler_params=pltpu.CompilerParams(
            collective_id=0, has_side_effects=True, vmem_limit_bytes=32 << 20
        ),
        name="features",
    )(*(pltpu.with_memory_space_constraint(v, pltpu.HBM) for v in (samples, frequencies, phases.reshape(1, 128))))
    return pl.pallas_call(
        gram_kernel,
        out_shape=jax.ShapeDtypeStruct((1024, 2048), F32),
        in_specs=[vmem] * 3,
        out_specs=hbm,
        scratch_shapes=[pltpu.VMEM((4, 1024, 128), F32), pltpu.SemaphoreType.DMA((28,))],
        compiler_params=pltpu.CompilerParams(vmem_limit_bytes=32 << 20),
        name="gram",
    )(left, right, gram)


def solution(mesh):
    in_specs = (P("row", None), P(None, ("row", "col")), P(("row", "col")))
    out_specs = P("row", "col")
    return jax.shard_map(body, mesh=mesh, in_specs=in_specs, out_specs=out_specs, check_vma=False)
```

time: 320 us -> 56.8 us (0.18)
  waiting for transfers between devices: 131 us -> 0 us
  matrix products: 125 us -> 0 us
  Pallas kernels: 0 us -> 56.5 us
  blocking collectives: 42.1 us -> 0 us
  between operations: 13.1 us -> 0.17 us
  other arithmetic: 8.52 us -> 0 us
    all_gather x3 -> x0, waiting for transfers between devices: 129 us -> none  [the longest x1 61.2 us: body(): lax.all_gather(frequencies, 'row', axis=1, tiled=True)]
    dot_general x8 -> x0, matrix products: 125 us -> none  [the longest x4 87.2 us: cross_product(): lax.dot_general(left_feats, right_feats, (((0,), (0,)), ((), ())), prefer...]
    pallas_call x0 -> x2, Pallas kernels: none -> 56.5 us  [the longest x1 52.9 us: body(): pl.pallas_call(functools.partial(features_kernel, 2.0 / total), out_shape...]
    all_gather x2 -> x0, blocking collectives: 42.1 us -> none  [the longest x1 26.8 us: body(): lax.all_gather(phases, 'row', axis=0, tiled=True)]
    mul x1 -> x0, other arithmetic: 8.44 us -> none  [body(): return gram_tile * (2.0 / total_samples)]
  transfers between devices with their start and end apart: 3 -> 0, of which waited for: 3 -> 0; matrix products, arithmetic and copies ran while one was open for 0% -> 0% of each run, Pallas kernels for 0% -> 0%
where the time goes in v2:
time: 56.8 us; the launch traced here: 56.6 us
  Pallas kernels  56.5 us (99%)
    pallas_call x1, Pallas kernels, body(): pl.pallas_call(functools.partial(features_kernel, 2.0 / total), out_shape...  52.9 us
    pallas_call x1, Pallas kernels, body(): pl.pallas_call(gram_kernel, out_shape=jax.ShapeDtypeStruct((1024, 2048),...  3.53 us

profile of v2, /device:TPU:1, one launch (start us, length us, event | category | flops | bytes accessed | tf_op | source)
XLA Modules:
  0.0 56.6 jit_solution(15458998381199762990)
XLA Ops:
  0.0 52.9 %features.1 = (bf16[1024,2048]{1,0:T(8,128)(2,1)S(1)}, bf16[16,2048,128]{2,1,0:T(8,128)(2,1)S(1)}, f32[16,1024,128]{2,1,0:T(8,128)S(1)}) custom-call(bf16[128,1024]{1,0:T(8,128)(2,1)} %samples.1, bf16[1024,128]{1,0:T(8,128)(2,1)} %freqs.1, bf16[1,128]{1,0:T(2,128)(2,1)} %bitcast.1), custom_call_target="tpu_custom_call" | custom-call | tf_op jit(solution)/shard_map/features/pallas_call | solution.py:279
  52.9 3.5 %gram.1 = f32[1024,2048]{1,0:T(8,128)} custom-call(bf16[1024,2048]{1,0:T(8,128)(2,1)S(1)} %get-tuple-element.8.left, bf16[16,2048,128]{2,1,0:T(8,128)(2,1)S(1)} %get-tuple-element.9.right, f32[16,1024,128]{2,1,0:T(8,128)S(1)} %get-tuple-element.10.gram), custom_call_target="tpu_custom_call" | custom-call | tf_op jit(solution)/shard_map/gram/pallas_call | solution.py:304

commit v3 on v2

--- a/solution.py
+++ b/solution.py
@@ -13,14 +13,15 @@
 MSG = 1040
 INV_TWO_PI = np.float32(1.0 / (2.0 * np.pi))
 SINE = (6.283164044230108, -41.33714235953727, 81.34076844401463, -70.99342854258839)
-PAIRS = ((0, 4), (1, 3), (2, 7), (5, 6))
+PAIRS = ((0, 3), (1, 2), (4, 7), (5, 6))
 STEPS = (
-    "LAs", "F0s", "L0s", "S0", "l0f+", "l0f-", "S-", "RXlo", "T0", "S+", "RXhi", "l0n", "SB0",
-    "N3b", "N1b", "R0s", "T3", "LA", "N2s", "F0", "N1s", "T2", "R4lo", "N2b", "N3s", "T1", "La2",
-    "l4f-", "R4hi", "La1", "La0", "r0f+", "r0f-", "l4f+", "A3", "P00", "l0l", "La3", "l4n", "r0n",
-    "P10", "A1", "La4", "T6", "T4", "T5", "l4l", "T7", "SB7", "Lb1", "Lb3", "r4f+", "A2", "L7",
-    "r4f-", "Lb0", "SB5", "Lb4", "Lb2", "r4n", "L5", "r0l", "SB6", "P20", "P21", "L6", "P11", "P01",
-    "Go0", "r4l", "SH1", "SH0", "SH2", "P30", "Go2", "P31", "SH3", "Go1", "Gs0", "Gs1", "Gs2",
+    "LAs", "F0s", "L0s", "S0", "RXhi", "l0f+", "l0f-", "S-", "S+", "N1b", "SB0", "l0n", "LA", "N3s",
+    "R0s", "T3", "F0", "T1", "T0", "N2s", "T2", "RXlo", "W3", "La3", "l0l", "N3b", "N1s", "T6",
+    "W2", "l4f-", "l4f+", "W0", "W4", "La2", "W1", "r0f+", "A1", "r0f-", "La0", "R4lo", "N2b",
+    "l4n", "r0n", "P00", "La1", "La4", "A3", "T5", "T4", "l4l", "R4hi", "T7", "SB5", "Lb0", "Lb2",
+    "Lb4", "W5", "A2", "r0l", "Lb3", "Lb5", "P10", "La5", "Lb1", "SB7", "r4f+", "r4f-", "r4n",
+    "P20", "SB6", "W7", "L7", "W6", "P01", "P21", "P11", "SH1", "SH0", "r4l", "SH2", "P31", "L6",
+    "Go2", "Go0", "Go1", "P30", "V2", "V1", "V0", "SH3", "Gs2", "Gs0", "Gs1",
 )
 LEFT_ORDER = ((0, 0), (1, 0), (0, 1), (0, 3), (1, 1), (1, 3), (0, 2), (1, 2))
 
@@ -226,6 +227,7 @@
     for i in range(8):
         step(f"T{i}", (), functools.partial(transpose, i))
     for b in range(8):
+        step(f"W{b}", (f"sib{b}",), None)
         step(f"La{b}", (f"sib{b}",), functools.partial(left_step, 0, 4, b))
         step(f"Lb{b}", (f"sib{b}",), functools.partial(left_step, 4, 4, b))
         step(f"L{b}", (f"sib{b}",), functools.partial(left_step, 0, 8, b))
@@ -235,6 +237,7 @@
         step(f"SH{i}", (), functools.partial(share, i))
         step(f"Go{i}", (), functools.partial(gram_step, i, k))
         step(f"Gs{i}", tuple(f"r{slot}" for slot in PAIRS[i]), functools.partial(gram_step, i, 1 - k))
+        step(f"V{i}", tuple(f"r{slot}" for slot in PAIRS[i]), None)
     for name in STEPS:
         steps[name]()
     shared(3)

time: 56.8 us -> 54.6 us (0.961)
  Pallas kernels: 56.5 us -> 54.3 us
    pallas_call x1, Pallas kernels: 52.9 us -> 50.8 us  [body(): pl.pallas_call(functools.partial(features_kernel, 2.0 / total), out_shape...]
where the time goes in v3:
time: 54.6 us; the launch traced here: 54.5 us
  Pallas kernels  54.3 us (99%)
    pallas_call x1, Pallas kernels, body(): pl.pallas_call(functools.partial(features_kernel, 2.0 / total), out_shape...  50.8 us
    pallas_call x1, Pallas kernels, body(): pl.pallas_call(gram_kernel, out_shape=jax.ShapeDtypeStruct((1024, 2048),...  3.53 us

profile of v3, /device:TPU:1, one launch (start us, length us, event | category | flops | bytes accessed | tf_op | source)
XLA Modules:
  0.0 54.5 jit_solution(8071803660032718409)
XLA Ops:
  0.0 50.8 %features.1 = (bf16[1024,2048]{1,0:T(8,128)(2,1)S(1)}, bf16[16,2048,128]{2,1,0:T(8,128)(2,1)S(1)}, f32[16,1024,128]{2,1,0:T(8,128)S(1)}) custom-call(bf16[128,1024]{1,0:T(8,128)(2,1)} %samples.1, bf16[1024,128]{1,0:T(8,128)(2,1)} %freqs.1, bf16[1,128]{1,0:T(2,128)(2,1)} %bitcast.1), custom_call_target="tpu_custom_call" | custom-call | tf_op jit(solution)/shard_map/features/pallas_call | solution.py:282
  50.8 3.5 %gram.1 = f32[1024,2048]{1,0:T(8,128)} custom-call(bf16[1024,2048]{1,0:T(8,128)(2,1)S(1)} %get-tuple-element.8.left, bf16[16,2048,128]{2,1,0:T(8,128)(2,1)S(1)} %get-tuple-element.9.right, f32[16,1024,128]{2,1,0:T(8,128)S(1)} %get-tuple-element.10.gram), custom_call_target="tpu_custom_call" | custom-call | tf_op jit(solution)/shard_map/gram/pallas_call | solution.py:307

commit v4 on v3

--- a/solution.py
+++ b/solution.py
@@ -21,7 +21,7 @@
     "l4n", "r0n", "P00", "La1", "La4", "A3", "T5", "T4", "l4l", "R4hi", "T7", "SB5", "Lb0", "Lb2",
     "Lb4", "W5", "A2", "r0l", "Lb3", "Lb5", "P10", "La5", "Lb1", "SB7", "r4f+", "r4f-", "r4n",
     "P20", "SB6", "W7", "L7", "W6", "P01", "P21", "P11", "SH1", "SH0", "r4l", "SH2", "P31", "L6",
-    "Go2", "Go0", "Go1", "P30", "V2", "V1", "V0", "SH3", "Gs2", "Gs0", "Gs1",
+    "Go2", "Go0", "Go1", "P30", "V2", "V1", "V0", "SH3", "Gs0", "Gs1",
 )
 LEFT_ORDER = ((0, 0), (1, 0), (0, 1), (0, 3), (1, 1), (1, 3), (0, 2), (1, 2))
 
@@ -257,18 +257,22 @@
         copy.start()
         copies.append(copy)
 
-    for pair in PAIRS[:-1]:
-        for core in range(2):
-            for slot in pair:
-                col = column(xh, z, core, slot)
-                write(gram.at[col], col, slice(0, 1024))
-    for core in range(2):
-        cols = [column(xh, z, core, slot) for slot in PAIRS[-1]]
+    done = [(i, core) for i in (0, 1) for core in (0, 1)] + [(2, k)]
+    for i, core in done:
+        for slot in PAIRS[i]:
+            col = column(xh, z, core, slot)
+            write(gram.at[col], col, slice(0, 1024))
+    for n, (i, core) in enumerate(((2, 1 - k), (3, 0), (3, 1))):
+        cols = [column(xh, z, core, slot) for slot in PAIRS[i]]
 
         def store(rows, acc):
             for d in range(2):
-                last[core * 2 + d, rows, :] = acc[:, d * 128:(d + 1) * 128]
-                write(last.at[core * 2 + d, rows, :], cols[d], rows)
+                last[n * 2 + d, rows, :] = acc[:, d * 128:(d + 1) * 128]
+            size = 512 if n == 2 else 1024
+            if rows.stop % size == 0:
+                ready = slice(rows.stop - size, rows.stop)
+                for d in range(2):
+                    write(last.at[n * 2 + d, ready, :], cols[d], ready)
 
         gram_pair(left, right, cols[0], cols[1], store)
     for copy in copies:
@@ -309,7 +313,7 @@
         out_shape=jax.ShapeDtypeStruct((1024, 2048), F32),
         in_specs=[vmem] * 3,
         out_specs=hbm,
-        scratch_shapes=[pltpu.VMEM((4, 1024, 128), F32), pltpu.SemaphoreType.DMA((28,))],
+        scratch_shapes=[pltpu.VMEM((6, 1024, 128), F32), pltpu.SemaphoreType.DMA((34,))],
         compiler_params=pltpu.CompilerParams(vmem_limit_bytes=32 << 20),
         name="gram",
     )(left, right, gram)

time: 54.6 us -> 54.6 us (level)
    pallas_call x1, Pallas kernels: 50.8 us -> 49.7 us  [body(): pl.pallas_call(functools.partial(features_kernel, 2.0 / total), out_shape...]
    pallas_call x1, Pallas kernels: 3.53 us -> 4.61 us  [body(): pl.pallas_call(gram_kernel, out_shape=jax.ShapeDtypeStruct((1024, 2048),...]
where the time goes in v4:
time: 54.6 us; the launch traced here: 54.4 us
  Pallas kernels  54.3 us (99%)
    pallas_call x1, Pallas kernels, body(): pl.pallas_call(functools.partial(features_kernel, 2.0 / total), out_shape...  49.7 us
    pallas_call x1, Pallas kernels, body(): pl.pallas_call(gram_kernel, out_shape=jax.ShapeDtypeStruct((1024, 2048),...  4.61 us

profile of v4, /device:TPU:1, one launch (start us, length us, event | category | flops | bytes accessed | tf_op | source)
XLA Modules:
  0.0 54.4 jit_solution(11500150453124514635)
XLA Ops:
  0.0 49.7 %features.1 = (bf16[1024,2048]{1,0:T(8,128)(2,1)S(1)}, bf16[16,2048,128]{2,1,0:T(8,128)(2,1)S(1)}, f32[16,1024,128]{2,1,0:T(8,128)S(1)}) custom-call(bf16[128,1024]{1,0:T(8,128)(2,1)} %samples.1, bf16[1024,128]{1,0:T(8,128)(2,1)} %freqs.1, bf16[1,128]{1,0:T(2,128)(2,1)} %bitcast.1), custom_call_target="tpu_custom_call" | custom-call | tf_op jit(solution)/shard_map/features/pallas_call | solution.py:286
  49.7 4.6 %gram.1 = f32[1024,2048]{1,0:T(8,128)} custom-call(bf16[1024,2048]{1,0:T(8,128)(2,1)S(1)} %get-tuple-element.8.left, bf16[16,2048,128]{2,1,0:T(8,128)(2,1)S(1)} %get-tuple-element.9.right, f32[16,1024,128]{2,1,0:T(8,128)S(1)} %get-tuple-element.10.gram), custom_call_target="tpu_custom_call" | custom-call | tf_op jit(solution)/shard_map/gram/pallas_call | solution.py:311
